TPU v7x, 32 devices: a whole 2x2x4 slice. The times are simulated.
32 devices in a mesh: req: 8 (over z, x), tp: 4 (over y, core).
Axes of the slice: x: 2, y: 2, z: 4, core: 2. Of those that a mesh axis runs over, the one named last changes fastest.
Arguments:
- tokens: bfloat16 [4096, 3584], P('req'), may hold values from -400 to 400, as said below
- norm_gain: float32 [3584], P(('req', 'tp')), may hold values from 0.5 to 1.5
- qkv_weight: float32 [3584, 4608], P(('req', 'tp')), may hold values from -0.09375 to 0.09375
- qkv_bias: float32 [4608], P(('req', 'tp')), may hold values from -48 to 48
- lengths: int32 [8, 4], P('req'), may hold values from 1 to 256, 512 in all within a row
Outputs:
- context: bfloat16 [4096, 3584], P('req', 'tp')
Inputs may be any that keep to these rules, and one draw needn't show every extreme that they name: `tokens`: hidden states of order one to some hundreds. Each replica's tenant lengths sum to 512, the largest is exactly 256.
All inputs are finite; a program needn't handle non-finite values.
Results may differ from a plain program's by a relative error of at most 0.009.
The roundings to bfloat16 on the way count: a program that leaves them out, or rounds other values in their place, can miss the bound.
Values may be sent and summed in bfloat16 or wider, within the bound.
A program may use at most 128 MiB of HBM per device.

v0:
```python
import math
import jax
import jax.numpy as jnp
from jax import lax
from jax.sharding import PartitionSpec as P

HEAD_DIM = 128
SINKS = 4
GROUP = 7
WINDOW = 160


def normalize(values, gain):
    wide = values.astype(jnp.float32)
    meansq = jnp.mean(wide * wide, axis=-1, keepdims=True)
    return (wide * lax.rsqrt(meansq + 1e-06) * gain.astype(jnp.float32)).astype(jnp.bfloat16)


def positions(lens, count):
    index = jnp.arange(count, dtype=jnp.int32)
    ends = jnp.cumsum(lens)
    after = index[:, None] >= ends[None, :]
    tenant = jnp.sum(after.astype(jnp.int32), axis=1)
    start = jnp.sum(jnp.where(after, lens[None, :], 0), axis=1)
    return (tenant, index - start)


def rotate(values, pos):
    half = HEAD_DIM // 2
    freqs = jnp.exp(-(jnp.arange(half, dtype=jnp.float32) * 2.0 / HEAD_DIM) * math.log(1000000.0))
    angle = pos.astype(jnp.float32)[:, None] * freqs[None, :]
    cosine = jnp.concatenate([jnp.cos(angle), jnp.cos(angle)], axis=-1)
    sine = jnp.concatenate([jnp.sin(angle), jnp.sin(angle)], axis=-1)
    shape = (values.shape[0],) + (1,) * (values.ndim - 2) + (HEAD_DIM,)
    cosine = cosine.reshape(shape)
    sine = sine.reshape(shape)
    turned = jnp.concatenate([-values[..., half:], values[..., :half]], axis=-1)
    return values * cosine + turned * sine


def attend(joined, tenant, pos):
    count = joined.shape[0]
    blocks = joined.reshape(count, -1, GROUP + 2, HEAD_DIM)
    query = rotate(blocks[:, :, :GROUP], pos).astype(jnp.bfloat16)
    key_part = rotate(blocks[:, :, GROUP], pos).astype(jnp.bfloat16)
    value_part = blocks[:, :, GROUP + 1].astype(jnp.bfloat16)
    scores = jnp.einsum(
        "qghd,kgd->ghqk", query, key_part, preferred_element_type=jnp.float32
    ) / math.sqrt(HEAD_DIM)
    same = tenant[:, None] == tenant[None, :]
    causal = pos[None, :] <= pos[:, None]
    near = jnp.logical_or(pos[:, None] - pos[None, :] < WINDOW, pos[None, :] < SINKS)
    allowed = jnp.logical_and(jnp.logical_and(same, causal), near)
    scores = jnp.where(allowed[None, None], scores, -1e30)
    peak = jnp.max(scores, axis=-1, keepdims=True)
    expo = jnp.where(allowed[None, None], jnp.exp(scores - peak), 0.0)
    weights = (expo / jnp.sum(expo, axis=-1, keepdims=True)).astype(jnp.bfloat16)
    mixed = jnp.einsum("ghqk,kgd->qghd", weights, value_part, preferred_element_type=jnp.float32)
    return mixed.reshape(count, -1).astype(jnp.bfloat16)


def shards(tokens, norm_gain, qkv_weight, qkv_bias, lengths):
    tp_count = lax.axis_size("tp")
    req_count = lax.axis_size("req")
    tp_place = lax.axis_index("tp")
    gain_full, bias_full = (
        lax.all_gather(norm_gain.astype(jnp.bfloat16), ("req", "tp"), axis=0, tiled=True),
        lax.all_gather(qkv_bias.astype(jnp.bfloat16), ("req", "tp"), axis=0, tiled=True),
    )
    width = bias_full.shape[0] // tp_count
    bias_block = lax.dynamic_slice_in_dim(bias_full, tp_place * width, width).astype(jnp.float32)
    normed = normalize(tokens, gain_full)
    weight_b = qkv_weight.astype(jnp.bfloat16)
    count = tokens.shape[0]
    gathered = lax.all_gather(weight_b, "req", axis=0, tiled=True)
    regrouped = lax.all_to_all(gathered, "tp", split_axis=1, concat_axis=0, tiled=True)
    shard_rows = weight_b.shape[0]
    reordered = (
        normed.reshape(count, req_count, tp_count, shard_rows)
        .transpose(0, 2, 1, 3)
        .reshape(count, -1)
    )
    joined = jnp.dot(reordered, regrouped, preferred_element_type=jnp.float32)
    joined = joined + bias_block[None, :]
    tenant, pos = positions(lengths[0], count)
    return attend(joined, tenant, pos)


def solution(mesh):
    placed = (
        P("req", None),
        P(("req", "tp")),
        P(("req", "tp"), None),
        P(("req", "tp")),
        P("req", None),
    )
    return jax.shard_map(
        shards, mesh=mesh, in_specs=placed, out_specs=P("req", "tp"), check_vma=False
    )
```

profile of v0, /device:TPU:0, one launch (start us, length us, event | category | flops | bytes accessed | tf_op | source)
XLA Modules:
  0.0 330.9 jit_solution(9403856503985649453)
XLA Ops:
  6.5 0.0 all-gather.2.cloned.1.call-start
  6.5 2.7 convert_element_type.70
  9.3 0.0 all-gather.2.cloned.1.call-update
  9.3 126.2 %all-gather.2.cloned.1.call-done = bf16[896,4608]{1,0:T(8,128)(2,1)} async-done(((bf16[112,4608]{1,0:T(8,128)(2,1)}), bf16[896,4608]{1,0:T(8,128)(2,1)}) %all-gather.2.cloned.1.call-update) | async-done | bytes 8257552 | tf_op jit(solution)/shard_map/all_gather | solution.py:75
  135.5 11.4 %copy.40 = bf16[896,4608]{0,1:T(8,128)(2,1)} copy(bf16[896,4608]{1,0:T(8,128)(2,1)} %all-gather.2.cloned.1.call-done) | data formatting | bytes 16515072 | tf_op jit(solution)/shard_map/all_gather | solution.py:75
  146.9 5.8 %all-to-all-start = ((bf16[896,4,1152]{0,2,1:T(8,128)(2,1)}), bf16[896,4,1152]{0,2,1:T(8,128)(2,1)}, u32[]{:S(2)}, u32[]{:S(2)}) async-start(bf16[896,4,1152]{0,2,1:T(8,128)(2,1)} %bitcast.65), calls=%async_computation | async-start | bytes 16515072 | tf_op jit(solution)/shard_map/all_to_all | solution.py:76
  152.7 0.0 copy-done.2
  152.7 0.0 copy-done.1
  152.7 0.0 copy-done
  152.7 0.2 reduce-window.8
  152.9 0.2 dynamic-update-slice
  153.1 0.2 dynamic-update-slice.1
  153.3 122.7 %all-reduce.2 = (bf16[3584]{0:T(1024)(128)(2,1)S(1)}, bf16[4608]{0:T(1024)(128)(2,1)S(1)}) all-reduce(bf16[3584]{0:T(1024)(128)(2,1)S(1)} %dynamic-update-slice, bf16[4608]{0:T(1024)(128)(2,1)S(1)} %dynamic-update-slice.1), channel_id=1, replica_groups=mesh['req'=8,'tp'=4] {'req','tp'}, use_global_device_ids=true, to_apply=%add | all-reduce | flops 8192 | bytes 32768
  276.0 5.9 %copy.38 = bf16[512,3584]{0,1:T(8,128)(2,1)} copy(bf16[512,3584]{1,0:T(8,128)(2,1)} %param.5) | data formatting | bytes 7340032 | tf_op args[0]
  282.0 2.9 fusion
  284.9 3.1 fusion.2
  288.0 2.0 copy.39
  290.0 0.1 dynamic-slice_convert_fusion
  290.1 0.1 convert_reduce_fusion
  290.2 0.5 fusion.27
  290.7 0.1 pad_maximum_fusion
  290.8 0.5 multiply_cosine_fusion.1
  291.3 0.4 fusion.14
  291.8 0.0 all-to-all-done
  291.8 11.5 %copy.41 = bf16[4,896,1152]{2,1,0:T(8,128)(2,1)} copy(bf16[4,896,1152]{1,2,0:T(8,128)(2,1)} %bitcast.4) | data formatting | bytes 16515072 | tf_op jit(solution)/shard_map/all_to_all | solution.py:76
  303.3 10.8 %convolution_add_fusion = f32[512,1152]{1,0:T(8,128)} fusion(bf16[512,3584]{0,1:T(8,128)(2,1)} %bitcast.72, bf16[3584,1152]{1,0:T(8,128)(2,1)} %bitcast.71, f32[1152]{0:T(1024)S(1)} %dynamic-slice_convert_fusion), kind=kOutput, calls=%fused_computation.13 | convolution fusion | flops 4228448256 | bytes 14291456 | tf_op jit(solution)/shard_map/dot_general | solution.py:83
  314.1 2.2 copy.42
  316.4 0.2 slice_negate_fusion
  316.6 1.7 fusion.3
  318.3 1.8 fusion.4
  320.1 2.7 fusion.10
  322.7 1.3 copy.46
  (14 shorter events, 0.1 us)
Async XLA Ops:
  6.5 128.9 %all-gather.2.cloned.1.call-start = ((), (), s32[]{:S(2)}) async-start(), calls=%async_computation.1 | async-start | bytes 9289728 | tf_op jit(solution)/shard_map/all_gather | solution.py:75
  146.9 5.8 %copy-start.2 = (f32[112]{0:T(128)S(1)}, f32[112]{0:T(128)}, u32[]{:S(2)}) copy-start(f32[112]{0:T(128)} %param.6) | copy-start | bytes 1348
  146.9 5.8 %copy-start.1 = (f32[144]{0:T(256)S(1)}, f32[144]{0:T(256)}, u32[]{:S(2)}) copy-start(f32[144]{0:T(256)} %param.8) | copy-start | bytes 1732
  146.9 5.8 %copy-start = (s32[1,4]{1,0:T(1,128)S(1)}, s32[1,4]{1,0:T(1,128)}, u32[]{:S(2)}) copy-start(s32[1,4]{1,0:T(1,128)} %param.9) | copy-start | bytes 52
  146.9 144.8 %all-to-all-start = ((bf16[896,4,1152]{0,2,1:T(8,128)(2,1)}), bf16[896,4,1152]{0,2,1:T(8,128)(2,1)}, u32[]{:S(2)}, u32[]{:S(2)}) async-start(bf16[896,4,1152]{0,2,1:T(8,128)(2,1)} %bitcast.65), calls=%async_computation | async-start | bytes 16515072 | tf_op jit(solution)/shard_map/all_to_all | solution.py:76
Sparse Core Ops, SparseCore 0:
  9.5 125.8 all-gather.1
where the time goes:
time: 332 us; the launch traced here: 331 us
  waiting for transfers between devices  126 us (38%)
  blocking collectives  123 us (37%)
  local copies, waits for them, and re-layouts  34.9 us (11%)
  matrix products  15.2 us (5%)
  between operations  13.6 us (4%)
  other arithmetic  12.6 us (4%)
  starting transfers between devices  5.76 us (2%)
    all_gather x1, waiting for transfers between devices, shards(): gathered = lax.all_gather(weight_b, 'req', axis=0, tiled=True)  126 us
    unnamed x1, blocking collectives  123 us
    all_to_all x1, local copies, waits for them, and re-layouts, shards(): lax.all_to_all(gathered, 'tp', split_axis=1, concat_axis=0, tiled=True)  11.5 us
    all_gather x1, local copies, waits for them, and re-layouts, shards(): gathered = lax.all_gather(weight_b, 'req', axis=0, tiled=True)  11.4 us
    dot_general x1, matrix products, shards(): joined = jnp.dot(reordered, regrouped, preferred_element_type=jnp.float32)  10.8 us
  transfers between devices with their start and end apart: 2, of which 1 were waited for; matrix products, arithmetic and copies ran while one was open for 5% of the time, Pallas kernels for 0%

commit v1 on v0

--- a/solution.py
+++ b/solution.py
@@ -73,7 +73,10 @@
     weight_b = qkv_weight.astype(jnp.bfloat16)
     count = tokens.shape[0]
     gathered = lax.all_gather(weight_b, "req", axis=0, tiled=True)
-    regrouped = lax.all_to_all(gathered, "tp", split_axis=1, concat_axis=0, tiled=True)
+    regrouped = jnp.concatenate(
+        lax.all_to_all(jnp.stack(jnp.split(gathered, lax.axis_size("tp"), axis=1)), "tp", 0, 0),
+        axis=0,
+    )
     shard_rows = weight_b.shape[0]
     reordered = (
         normed.reshape(count, req_count, tp_count, shard_rows)

time: 332 us -> 316 us (0.952)
  local copies, waits for them, and re-layouts: 34.9 us -> 15.7 us
  other arithmetic: 12.6 us -> 16.5 us
    all_to_all x1 -> x0, local copies, waits for them, and re-layouts: 11.5 us -> none  [shards(): lax.all_to_all(gathered, 'tp', split_axis=1, concat_axis=0, tiled=True)]
    all_gather x1 -> x0, local copies, waits for them, and re-layouts: 11.4 us -> none  [shards(): gathered = lax.all_gather(weight_b, 'req', axis=0, tiled=True)]
    another operation x1 -> x2, other arithmetic: 0.18 us -> 4.1 us  [the longest x1 3.93 us: shards(): jnp.stack(jnp.split(gathered, lax.axis_size('tp'), axis=1))]
    another operation x0 -> x1, local copies, waits for them, and re-layouts: none -> 3.74 us  [shards(): jnp.stack(jnp.split(gathered, lax.axis_size('tp'), axis=1))]
where the time goes in v1:
time: 316 us
  waiting for transfers between devices  126 us (40%)
  blocking collectives  123 us (39%)
  other arithmetic  16.5 us (5%)
  local copies, waits for them, and re-layouts  15.7 us (5%)
  matrix products  15.2 us (5%)
  between operations  13.6 us (4%)
  starting transfers between devices  5.75 us (2%)
    all_gather x1, waiting for transfers between devices, shards(): gathered = lax.all_gather(weight_b, 'req', axis=0, tiled=True)  126 us
    unnamed x1, blocking collectives  123 us
    dot_general x1, matrix products, shards(): joined = jnp.dot(reordered, regrouped, preferred_element_type=jnp.float32)  10.9 us
    unnamed x11, local copies, waits for them, and re-layouts  6.44 us
  transfers between devices with their start and end apart: 2, of which 1 were waited for; matrix products, arithmetic and copies ran while one was open for 5% of the time, Pallas kernels for 0%

profile of v1, /device:TPU:0, one launch (start us, length us, event | category | flops | bytes accessed | tf_op | source)
XLA Modules:
  0.0 315.8 jit_solution(1374675945641218322)
XLA Ops:
  6.5 0.0 all-gather.2.cloned.1.call-start
  6.5 2.7 convert_element_type.70
  9.3 0.0 all-gather.2.cloned.1.call-update
  9.3 126.2 %all-gather.2.cloned.1.call-done = bf16[896,4608]{1,0:T(8,128)(2,1)} async-done(((bf16[112,4608]{1,0:T(8,128)(2,1)}), bf16[896,4608]{1,0:T(8,128)(2,1)}) %all-gather.2.cloned.1.call-update) | async-done | bytes 8257552 | tf_op jit(solution)/shard_map/all_gather | solution.py:75
  135.5 3.7 %slice_bitcast_fusion.3 = (bf16[1,896,1152]{2,1,0:T(8,128)(2,1)S(1)}, bf16[1,896,1152]{2,1,0:T(8,128)(2,1)S(1)}, bf16[1,896,1152]{2,1,0:T(8,128)(2,1)S(1)}, bf16[1,896,1152]{2,1,0:T(8,128)(2,1)S(1)}) fusion(bf16[896,4608]{1,0:T(8,128)(2,1)} %all-gather.2.cloned.1.call-done), kind=kLoop, calls=%fused_computation.18 | loop fusion | bytes 16515072 | tf_op jit(solution)/shard_map/stack | solution.py:77
  139.2 3.9 %pad_maximum_fusion = bf16[4,896,1152]{2,1,0:T(8,128)(2,1)} fusion(bf16[1,896,1152]{2,1,0:T(8,128)(2,1)S(1)} %get-tuple-element.10, bf16[1,896,1152]{2,1,0:T(8,128)(2,1)S(1)} %get-tuple-element.11, bf16[1,896,1152]{2,1,0:T(8,128)(2,1)S(1)} %get-tuple-element.12, bf16[1,896,1152]{2,1,0:T(8,128)(2,1)S(1)} %get-tuple-element.9), kind=kLoop, calls=%fused_computation.2 | loop fusion | flops 12386304 | bytes 16515072 | tf_op jit(solution)/shard_map/stack | solution.py:77
  143.2 5.8 %all-to-all-start = ((bf16[4,896,1152]{2,1,0:T(8,128)(2,1)}), bf16[4,896,1152]{2,1,0:T(8,128)(2,1)}, u32[]{:S(2)}, u32[]{:S(2)}) async-start(bf16[4,896,1152]{2,1,0:T(8,128)(2,1)} %pad_maximum_fusion), calls=%async_computation | async-start | bytes 16515072 | tf_op jit(solution)/shard_map/all_to_all | solution.py:77
  148.9 0.0 copy-done.1
  149.0 0.0 copy-done.2
  149.0 0.2 dynamic-update-slice.1
  149.2 0.2 dynamic-update-slice
  149.5 122.8 %all-reduce.2 = (bf16[3584]{0:T(1024)(128)(2,1)S(1)}, bf16[4608]{0:T(1024)(128)(2,1)S(1)}) all-reduce(bf16[3584]{0:T(1024)(128)(2,1)S(1)} %dynamic-update-slice, bf16[4608]{0:T(1024)(128)(2,1)S(1)} %dynamic-update-slice.1), channel_id=1, replica_groups=mesh['req'=8,'tp'=4] {'req','tp'}, use_global_device_ids=true, to_apply=%add | all-reduce | flops 8192 | bytes 32768
  272.3 5.9 %copy.20 = bf16[512,3584]{0,1:T(8,128)(2,1)} copy(bf16[512,3584]{1,0:T(8,128)(2,1)} %param.5) | data formatting | bytes 7340032 | tf_op args[0]
  278.2 2.9 fusion
  281.1 3.1 fusion.2
  284.2 2.0 copy.21
  286.3 0.0 copy-done
  286.3 0.2 reduce-window.8
  286.4 0.1 dynamic-slice_convert_fusion
  286.5 0.1 convert_reduce_fusion
  286.6 0.5 fusion.27
  287.2 0.1 pad_maximum_fusion.1
  287.2 0.5 multiply_cosine_fusion.1
  287.7 0.4 fusion.14
  288.2 0.0 all-to-all-done
  288.2 10.9 %convolution_add_fusion = f32[512,1152]{1,0:T(8,128)} fusion(bf16[512,3584]{0,1:T(8,128)(2,1)} %bitcast.76, bf16[3584,1152]{1,0:T(8,128)(2,1)} %bitcast.7, f32[1152]{0:T(1024)S(1)} %dynamic-slice_convert_fusion), kind=kOutput, calls=%fused_computation.14 | convolution fusion | flops 4228448256 | bytes 14291456 | tf_op jit(solution)/shard_map/dot_general | solution.py:86
  299.1 2.2 copy.22
  301.3 0.2 slice_negate_fusion
  301.6 1.6 fusion.3
  303.2 1.8 fusion.4
  305.0 2.7 fusion.10
  307.7 1.3 copy.26
  (14 shorter events, 0.1 us)
Async XLA Ops:
  6.5 128.9 %all-gather.2.cloned.1.call-start = ((), (), s32[]{:S(2)}) async-start(), calls=%async_computation.1 | async-start | bytes 9289728 | tf_op jit(solution)/shard_map/all_gather | solution.py:75
  143.2 5.8 %copy-start.1 = (f32[144]{0:T(256)S(1)}, f32[144]{0:T(256)}, u32[]{:S(2)}) copy-start(f32[144]{0:T(256)} %param.8) | copy-start | bytes 1732
  143.2 5.8 %copy-start.2 = (f32[112]{0:T(128)S(1)}, f32[112]{0:T(128)}, u32[]{:S(2)}) copy-start(f32[112]{0:T(128)} %param.6) | copy-start | bytes 1348
  143.2 145.0 %all-to-all-start = ((bf16[4,896,1152]{2,1,0:T(8,128)(2,1)}), bf16[4,896,1152]{2,1,0:T(8,128)(2,1)}, u32[]{:S(2)}, u32[]{:S(2)}) async-start(bf16[4,896,1152]{2,1,0:T(8,128)(2,1)} %pad_maximum_fusion), calls=%async_computation | async-start | bytes 16515072 | tf_op jit(solution)/shard_map/all_to_all | solution.py:77
  281.1 5.1 %copy-start = (s32[1,4]{1,0:T(1,128)S(1)}, s32[1,4]{1,0:T(1,128)}, u32[]{:S(2)}) copy-start(s32[1,4]{1,0:T(1,128)} %param.9) | copy-start | bytes 52
Sparse Core Ops, SparseCore 0:
  9.5 125.8 all-gather.1
